TPU v7x, 32 devices: a whole 2x2x4 slice. The times are simulated.
32 devices in a mesh: dp: 8 (over z, x), seq: 4 (over y, core).
Axes of the slice: x: 2, y: 2, z: 4, core: 2. Of those that a mesh axis runs over, the one named last changes fastest.
Arguments:
- layer_in: bfloat16 [8192, 2048], P(('dp', 'seq')), may hold values from -6 to 6
- out_grad: bfloat16 [8192, 2048], P(('dp', 'seq')), may hold values from -6 to 6
- seq_start: int32 [8, 4], P('dp'), may hold values from 0 to 1, as said below
- norm1_gain: bfloat16 [2048], P(('dp', 'seq')), may hold values from 0.25 to 1.75
- norm1_shift: bfloat16 [2048], P(('dp', 'seq')), may hold values from -3 to 3
- proj_in: bfloat16 [2048, 12288], P(('dp', 'seq')), may hold values from -0.125 to 0.125
- proj_out: bfloat16 [4096, 2048], P(('dp', 'seq')), may hold values from -0.125 to 0.125
- norm2_gain: bfloat16 [2048], P(('dp', 'seq')), may hold values from 0.25 to 1.75
- norm2_shift: bfloat16 [2048], P(('dp', 'seq')), may hold values from -3 to 3
- ffn_up: bfloat16 [2048, 4096], P(('dp', 'seq')), may hold values from -0.125 to 0.125
- ffn_down: bfloat16 [4096, 2048], P(('dp', 'seq')), may hold values from -0.125 to 0.125
Outputs:
- layer_out: bfloat16 [8192, 2048], P(('dp', 'seq'))
- in_grad: bfloat16 [8192, 2048], P(('dp', 'seq'))
- norm1_gain_grad: float32 [2048], P(('dp', 'seq'))
- norm1_shift_grad: float32 [2048], P(('dp', 'seq'))
- proj_in_grad: float32 [2048, 12288], P(('dp', 'seq'))
- proj_out_grad: float32 [4096, 2048], P(('dp', 'seq'))
- norm2_gain_grad: float32 [2048], P(('dp', 'seq'))
- norm2_shift_grad: float32 [2048], P(('dp', 'seq'))
- ffn_up_grad: float32 [2048, 4096], P(('dp', 'seq'))
- ffn_down_grad: float32 [4096, 2048], P(('dp', 'seq'))
Inputs may be any that keep to these rules, and one draw needn't show every extreme that they name: `seq_start`: each group's first block is 1, and a 1 stands only at even block indices, so every sequence covers an even number of blocks of 256 tokens.
All inputs are finite; a program needn't handle non-finite values.
Results may differ from a plain program's by a relative error of at most 0.014.
The roundings to bfloat16 on the way count: a program that leaves them out, or rounds other values in their place, can miss the bound.
Values may be sent and summed in bfloat16 or wider, within the bound.
No kernel may reach another device: no remote copies, remote signals or barrier semaphores. Data moves between devices by JAX's collectives and lax.ppermute only.
A program may use at most 336 MiB of HBM per device.

v0:
```python
import jax
import jax.numpy as jnp
from jax import lax
from jax.sharding import PartitionSpec as P

D = 2048
HEADS = 8
VD = 4096
DK = 256
DV = 512
BOTH = ("dp", "seq")
f32 = jnp.float32
bf16 = jnp.bfloat16


def layer_norm(rows, row_gain, row_shift):
    average = jnp.mean(rows, axis=-1, keepdims=True)
    centred = rows - average
    spread = jnp.mean(centred * centred, axis=-1, keepdims=True)
    return centred * lax.rsqrt(spread + 1e-05) * row_gain + row_shift


def gate_norm(gate_pre, retained):
    average = jnp.mean(retained, axis=-1, keepdims=True)
    centred = retained - average
    spread = jnp.maximum(jnp.mean(centred * centred, axis=-1, keepdims=True), 0.25)
    normed = centred * lax.rsqrt(spread + 1e-05)
    swish = gate_pre * jax.nn.sigmoid(gate_pre)
    return swish * normed


def gelu_exact(values):
    return jax.nn.gelu(values, approximate=False)


def rotate(heads_in, cosine, sine):
    half_width = heads_in.shape[-1] // 2
    first = heads_in[..., :half_width]
    second = heads_in[..., half_width:]
    return jnp.concatenate(
        [first * cosine - second * sine, first * sine + second * cosine], axis=-1
    )


def dot(a, b, dims):
    return lax.dot_general(a, b, (dims, ((), ())), preferred_element_type=f32)


def seq_bits(size):
    return [1 << b for b in range(size.bit_length() - 1)]


def swap_seq(x, bit):
    size = lax.axis_size("seq")
    return lax.ppermute(x, "seq", [(i, i ^ bit) for i in range(size)])


def gather_seq(x):
    size, me = (lax.axis_size("seq"), lax.axis_index("seq"))
    held = x[None]
    for bit in reversed(seq_bits(size)):
        other = swap_seq(held, bit)
        upper = me & bit != 0
        held = jnp.where(upper, jnp.stack([other, held]), jnp.stack([held, other]))
        held = held.reshape((-1,) + x.shape) if bit == size // 2 else held
        if bit != size // 2:
            held = jnp.swapaxes(held, 0, 1).reshape((-1,) + x.shape)
    return held


def scatter_seq(x):
    size, me = (lax.axis_size("seq"), lax.axis_index("seq"))
    held = x
    for bit in seq_bits(size):
        pairs = held.reshape((held.shape[0] // 2, 2) + held.shape[1:])
        mine = jnp.where(me & bit != 0, 1, 0)
        keep = lax.dynamic_index_in_dim(pairs, mine, 1, False)
        give = lax.dynamic_index_in_dim(pairs, 1 - mine, 1, False)
        held = keep.astype(f32) + swap_seq(give.astype(bf16), bit).astype(f32)
    return held[0]


def exchange_seq(x):
    return lax.all_to_all(x, "seq", 0, 0)


def gather_dp(x):
    return lax.all_gather(x, "dp", axis=0, tiled=True)


def scatter_dp(x):
    return lax.psum_scatter(x.astype(bf16), "dp", scatter_dimension=0, tiled=True)


def local(
    layer_in,
    out_grad,
    seq_start,
    norm1_gain,
    norm1_shift,
    proj_in,
    proj_out,
    norm2_gain,
    norm2_shift,
    ffn_up,
    ffn_down,
):
    S, G = (lax.axis_size("seq"), lax.axis_size("dp"))
    me = lax.axis_index("seq")
    T = layer_in.shape[0]
    TG = S * T
    H = HEADS // S
    QW, VW = (H * DK, H * DV)
    FR = ffn_down.shape[0]
    FW = G * FR
    norms = lax.all_gather(
        jnp.stack([norm1_gain, norm1_shift, norm2_gain, norm2_shift]), BOTH, axis=1, tiled=True
    ).astype(f32)
    gain_one, shift_one, gain_two, shift_two = norms
    rows_in = proj_in.shape[0]
    pieces = []
    start = 0
    for width in (QW, QW, VW, VW):
        part = proj_in[:, start : start + S * width]
        pieces.append(part.reshape(rows_in, S, width))
        start += S * width
    w_in = jnp.concatenate(pieces, axis=2).transpose(1, 0, 2)
    w_in = exchange_seq(w_in).reshape(S * rows_in, 2 * QW + 2 * VW)
    w_in = gather_dp(w_in)
    w_out = lax.ppermute(
        proj_out, BOTH, [(j * G + t, t * S + j) for j in range(S) for t in range(G)]
    )
    w_out = gather_dp(w_out)
    rows_up = ffn_up.shape[0]
    w_up = ffn_up.reshape(rows_up, G, S, FR).transpose(2, 0, 1, 3).reshape(S, rows_up, FW)
    w_up = gather_dp(exchange_seq(w_up).reshape(S * rows_up, FW))
    w_down = gather_dp(ffn_down)
    rows_full = layer_in.astype(f32)
    normed_one, norm1_back = jax.vjp(layer_norm, rows_full, gain_one, shift_one)
    hidden_one = gather_seq(normed_one.astype(bf16)).reshape(TG, D)
    cot = gather_seq(out_grad).reshape(TG, D)
    projected = dot(hidden_one, w_in, ((1,), (0,)))
    q_pre = projected[:, :QW].reshape(S, T, H, DK)
    k_pre = projected[:, QW : 2 * QW].reshape(S, T, H, DK)
    values = projected[:, 2 * QW : 2 * QW + VW].astype(bf16).reshape(S, T, H, DV)
    gate_pre = projected[:, 2 * QW + VW :].reshape(S, T, H, DV)
    half = DK // 2
    factor = jnp.power(10000.0, -jnp.arange(half, dtype=f32) / (half - 1))
    angles = jnp.arange(TG, dtype=f32)[:, None] * factor[None, :]
    cosine = jnp.cos(angles).reshape(S, T, 1, half)
    sine = jnp.sin(angles).reshape(S, T, 1, half)
    key_scale = DK ** (-0.5)
    queries = rotate(q_pre, cosine, sine).astype(bf16)
    keys = (rotate(k_pre, cosine, sine) * key_scale).astype(bf16)
    log_all = jnp.log(1.0 - jnp.exp2(-5.0 - jnp.arange(HEADS, dtype=f32)))
    log_decay = lax.dynamic_slice_in_dim(log_all, me * H, H)
    steps = jnp.arange(T, dtype=f32)
    decay_query = jnp.exp((steps + 1.0)[:, None] * log_decay[None, :])
    decay_key = jnp.exp((T - 1.0 - steps)[:, None] * log_decay[None, :])
    distance = steps[:, None] - steps[None, :]
    lower = distance[None] >= 0.0
    safe = jnp.where(lower, distance[None], 0.0)
    mask = jnp.where(lower, jnp.exp(safe * log_decay[:, None, None]), 0.0)
    block_decay = jnp.exp(T * log_decay)[:, None, None]
    keep = 1.0 - seq_start[0].astype(f32)
    query_decay = (queries.astype(f32) * decay_query[None, :, :, None]).astype(bf16)
    key_decay = (keys.astype(f32) * decay_key[None, :, :, None]).astype(bf16)

    def ein(spec, a, b):
        return jnp.einsum(spec, a, b, preferred_element_type=f32)

    raw = ein("bihd,bjhd->bhij", queries, keys)
    scores = (raw * mask[None]).astype(bf16)
    local_state = ein("bjhd,bjhe->bhde", key_decay, values)
    carry = jnp.zeros_like(local_state[0])
    states = []
    for b in range(S):
        state = keep[b] * carry
        states.append(state.astype(bf16))
        carry = block_decay * state + local_state[b]
    state_in = jnp.stack(states)
    retained = ein("bhij,bjhe->bihe", scores, values) + ein(
        "bihd,bhde->bihe", query_decay, state_in
    )
    gated, gate_back = jax.vjp(gate_norm, gate_pre, retained)
    mixed = gated.astype(bf16).reshape(TG, VW)
    attn = scatter_seq(dot(mixed, w_out, ((1,), (0,))).reshape(S, T, D))
    middle = rows_full + attn
    normed_two, norm2_back = jax.vjp(layer_norm, middle, gain_two, shift_two)
    hidden_two = gather_seq(normed_two.astype(bf16)).reshape(TG, D)
    up_pre = dot(hidden_two, w_up, ((1,), (0,)))
    active_full, gelu_back = jax.vjp(gelu_exact, up_pre)
    active = active_full.astype(bf16)
    down = scatter_seq(dot(active, w_down, ((1,), (0,))).reshape(S, T, D))
    layer_out = (middle + down).astype(bf16)
    down_grad = scatter_dp(dot(active, cot, ((0,), (0,)))).astype(f32)
    grad_active = dot(cot, w_down, ((1,), (1,)))
    grad_up = gelu_back(grad_active)[0].astype(bf16)
    up_grad = scatter_dp(dot(hidden_two, grad_up, ((0,), (0,))))
    up_grad = exchange_seq(up_grad.reshape(S, rows_up, FW)).reshape(S, rows_up, G, FR)
    up_grad = up_grad.transpose(1, 2, 0, 3).reshape(rows_up, G * S * FR).astype(f32)
    grad_hidden_two = scatter_seq(dot(grad_up, w_up, ((1,), (1,))).reshape(S, T, D))
    grad_mid_part, gain_two_grad, shift_two_grad = norm2_back(grad_hidden_two)
    grad_middle = out_grad.astype(f32) + grad_mid_part
    grad_attn = gather_seq(grad_middle.astype(bf16)).reshape(TG, D)
    out_term = scatter_dp(dot(mixed, grad_attn, ((0,), (0,))))
    out_grad_w = lax.ppermute(
        out_term, BOTH, [(t * S + j, j * G + t) for j in range(S) for t in range(G)]
    ).astype(f32)
    grad_mixed = dot(grad_attn, w_out, ((1,), (1,))).reshape(S, T, H, DV)
    grad_gate, grad_ret = gate_back(grad_mixed)
    grad_gate = grad_gate.astype(bf16)
    grad_ret = grad_ret.astype(bf16)
    grad_qdecay = ein("bihe,bhde->bihd", grad_ret, state_in)
    state_grad = ein("bihd,bihe->bhde", query_decay, grad_ret)
    grad_scores = ein("bihe,bjhe->bhij", grad_ret, values)
    grad_raw = (grad_scores * mask[None]).astype(bf16)
    later = jnp.zeros_like(state_grad[0])
    laters = [None] * S
    for b in reversed(range(S)):
        laters[b] = later.astype(bf16)
        later = keep[b] * (state_grad[b] + block_decay * later)
    grad_local = jnp.stack(laters)
    grad_query = (
        ein("bhij,bjhd->bihd", grad_raw, keys) + grad_qdecay * decay_query[None, :, :, None]
    )
    grad_key = (
        ein("bhij,bihd->bjhd", grad_raw, queries)
        + ein("bjhe,bhde->bjhd", values, grad_local) * decay_key[None, :, :, None]
    )
    grad_value = ein("bhij,bihe->bjhe", scores, grad_ret) + ein(
        "bjhd,bhde->bjhe", key_decay, grad_local
    )
    grad_qpre = rotate(grad_query, cosine, -sine).astype(bf16).reshape(TG, QW)
    grad_kpre = rotate(grad_key * key_scale, cosine, -sine).astype(bf16).reshape(TG, QW)
    grad_projected = jnp.concatenate(
        [grad_qpre, grad_kpre, grad_value.astype(bf16).reshape(TG, VW), grad_gate.reshape(TG, VW)],
        axis=1,
    )
    in_term = scatter_dp(dot(hidden_one, grad_projected, ((0,), (0,))))
    in_term = exchange_seq(in_term.reshape(S, rows_in, 2 * QW + 2 * VW))
    cols = []
    start = 0
    for width in (QW, QW, VW, VW):
        part = in_term[:, :, start : start + width]
        cols.append(part.transpose(1, 0, 2).reshape(rows_in, S * width))
        start += width
    in_grad_w = jnp.concatenate(cols, axis=1).astype(f32)
    grad_hidden_one = scatter_seq(dot(grad_projected, w_in, ((1,), (1,))).reshape(S, T, D))
    grad_in_part, gain_one_grad, shift_one_grad = norm1_back(grad_hidden_one)
    in_grad = (grad_middle + grad_in_part).astype(bf16)
    norm_grads = lax.psum_scatter(
        jnp.stack([gain_one_grad, shift_one_grad, gain_two_grad, shift_two_grad]),
        BOTH,
        scatter_dimension=1,
        tiled=True,
    )
    return (
        layer_out,
        in_grad,
        norm_grads[0],
        norm_grads[1],
        in_grad_w,
        out_grad_w,
        norm_grads[2],
        norm_grads[3],
        up_grad,
        down_grad,
    )


def solution(mesh):
    rows, vector = (P(BOTH, None), P(BOTH))
    in_specs = (rows, rows, P("dp", None), vector, vector, rows, rows, vector, vector, rows, rows)
    out_specs = (rows, rows, vector, vector, rows, rows, vector, vector, rows, rows)
    return jax.shard_map(local, mesh=mesh, in_specs=in_specs, out_specs=out_specs, check_vma=False)
```

profile of v0, /device:TPU:0, one launch (start us, length us, event | category | flops | bytes accessed | tf_op | source)
XLA Modules:
  0.0 1129.7 jit_solution(7035085313268230148)
XLA Ops:
  12.0 24.4 %all_to_all.20 = bf16[4,64,3072]{2,1,0:T(8,128)(2,1)} all-to-all(bf16[4,64,3072]{2,1,0:T(8,128)(2,1)S(1)} %copy.198), channel_id=1, replica_groups=mesh['dp'=8,'seq'=4] {'seq'}, dimensions={0} | all-to-all | bytes 3145728 | tf_op jit(solution)/shard_map/all_to_all | solution.py:84
  38.0 106.0 %all-gather = bf16[32,64,4]{1,2,0:T(4,128)(2,1)S(1)} all-gather(bf16[1,64,4]{1,2,0:T(4,128)(2,1)S(1)} %maximum_bitcast_fusion.1), channel_id=1, replica_groups=mesh['dp'=8,'seq'=4] {'dp','seq'}, dimensions={0}, use_global_device_ids=true | all-gather | bytes 16896 | tf_op jit(solution)/shard_map/all_gather | solution.py:116
  153.1 4.1 all-to-all-start.1
  157.3 15.8 %collective-permute-done = bf16[1,256,2048]{2,1,0:T(8,128)(2,1)S(1)} collective-permute-done((bf16[1,256,2048]{2,1,0:T(8,128)(2,1)}, bf16[1,256,2048]{2,1,0:T(8,128)(2,1)S(1)}, u32[]{:S(2)}, u32[]{:S(2)}) %collective-permute-start) | collective-permute-done | bytes 1048608 | tf_op jit(solution)/shard_map/ppermute | solution.py:55
  173.1 3.3 maximum_select_fusion.4
  179.5 3.1 fusion.58
  183.3 2.8 fusion.4
  186.1 2.3 copy.197
  188.4 51.1 %all-gather.6.cloned.1.call-done = bf16[2048,3072]{1,0:T(8,128)(2,1)} async-done(((bf16[256,3072]{1,0:T(8,128)(2,1)}), bf16[2048,3072]{1,0:T(8,128)(2,1)}) %all-gather.6.cloned.1.call-update) | async-done | bytes 12582928 | tf_op jit(solution)/shard_map/all_gather | solution.py:88
  239.5 17.0 %fusion.85 = f32[1024,3072]{1,0:T(8,128)S(1)} fusion(bf16[1024,2048]{1,0:T(8,128)(2,1)} %bitcast.265, bf16[2048,3072]{1,0:T(8,128)(2,1)} %all-gather.6.cloned.1.call-done), kind=kOutput, calls=%fused_computation.220 | convolution fusion | flops 12884901888 | bytes 29360128 | tf_op jit(solution)/shard_map/dot_general | solution.py:46
  260.4 2.4 fusion.77
  262.8 3.3 reshape.733
  266.1 4.3 reshape.734
  270.5 6.7 reshape.732
  277.2 7.2 copy.200
  284.4 3.7 reshape.735
  288.1 2.6 fusion.78
  292.6 2.5 fusion.68
  303.1 10.7 all-gather.8.cloned.1.call-done
  313.8 6.4 fusion.8
  324.2 4.4 collective-permute-done.3
  328.5 2.8 bitcast_add_fusion.3
  335.7 23.9 %collective-permute-done.4 = bf16[1,256,2048]{2,1,0:T(8,128)(2,1)} collective-permute-done((bf16[1,256,2048]{2,1,0:T(8,128)(2,1)S(1)}, bf16[1,256,2048]{2,1,0:T(8,128)(2,1)}, u32[]{:S(2)}, u32[]{:S(2)}) %collective-permute-start.4) | collective-permute-done | bytes 1048608 | tf_op jit(solution)/shard_map/ppermute | solution.py:55
  359.7 2.3 fusion.76
  364.4 17.7 %collective-permute-done.9 = bf16[1,256,2048]{2,1,0:T(8,128)(2,1)S(1)} collective-permute-done((bf16[1,256,2048]{2,1,0:T(8,128)(2,1)}, bf16[1,256,2048]{2,1,0:T(8,128)(2,1)S(1)}, u32[]{:S(2)}, u32[]{:S(2)}) %collective-permute-start.9) | collective-permute-done | bytes 1048608 | tf_op jit(solution)/shard_map/ppermute | solution.py:55
  384.1 19.6 %collective-permute-done.5 = bf16[1,256,2048]{2,1,0:T(8,128)(2,1)S(1)} collective-permute-done((bf16[1,256,2048]{2,1,0:T(8,128)(2,1)S(1)}, bf16[1,256,2048]{2,1,0:T(8,128)(2,1)S(1)}, u32[]{:S(2)}, u32[]{:S(2)}) %collective-permute-start.5) | collective-permute-done | bytes 1048608 | tf_op jit(solution)/shard_map/ppermute | solution.py:55
  411.0 2.3 copy.210
  413.4 9.9 fusion.86
  423.2 38.1 %all-gather.12.cloned.1.call-done = bf16[1024,2048]{1,0:T(8,128)(2,1)} async-done(((bf16[128,2048]{1,0:T(8,128)(2,1)}), bf16[1024,2048]{1,0:T(8,128)(2,1)}) %all-gather.12.cloned.1.call-update) | async-done | bytes 4194320 | tf_op jit(solution)/shard_map/all_gather | solution.py:88
  461.3 16.9 %add_convert_fusion.2 = (bf16[1024,1024]{1,0:T(8,128)(2,1)S(1)}, f32[1024,1024]{1,0:T(8,128)S(1)}) fusion(f32[1024,1024]{1,0:T(8,128)} %fusion.86, bf16[1024,2048]{1,0:T(8,128)(2,1)} %bitcast.269, bf16[1024,2048]{1,0:T(8,128)(2,1)} %all-gather.12.cloned.1.call-done), kind=kOutput, calls=%fused_computation.31 | convolution fusion | flops 4370464768 | bytes 18874368 | tf_op jit(solution)/shard_map/dot_general | solution.py:46
  478.2 2.5 multiply_convert_fusion
  481.9 6.2 convolution_convert_fusion.2
  488.2 7.3 fusion.88
  497.1 4.5 fusion.87
  506.3 2.5 bitcast_add_fusion.2
  510.5 18.6 %collective-permute-done.12 = bf16[1,256,2048]{2,1,0:T(8,128)(2,1)S(1)} collective-permute-done((bf16[1,256,2048]{2,1,0:T(8,128)(2,1)S(1)}, bf16[1,256,2048]{2,1,0:T(8,128)(2,1)S(1)}, u32[]{:S(2)}, u32[]{:S(2)}) %collective-permute-start.12) | collective-permute-done | bytes 1048608 | tf_op jit(solution)/shard_map/ppermute | solution.py:55
  529.9 21.3 %collective-permute-done.8 = bf16[1,256,2048]{2,1,0:T(8,128)(2,1)S(1)} collective-permute-done((bf16[1,256,2048]{2,1,0:T(8,128)(2,1)S(1)}, bf16[1,256,2048]{2,1,0:T(8,128)(2,1)S(1)}, u32[]{:S(2)}, u32[]{:S(2)}) %collective-permute-start.8) | collective-permute-done | bytes 1048608 | tf_op jit(solution)/shard_map/ppermute | solution.py:55
  553.1 2.4 fusion.124
  557.0 23.3 %collective-permute-done.13 = bf16[1,256,2048]{2,1,0:T(8,128)(2,1)S(1)} collective-permute-done((bf16[1,256,2048]{2,1,0:T(8,128)(2,1)S(1)}, bf16[1,256,2048]{2,1,0:T(8,128)(2,1)S(1)}, u32[]{:S(2)}, u32[]{:S(2)}) %collective-permute-start.13) | collective-permute-done | bytes 1048608 | tf_op jit(solution)/shard_map/ppermute | solution.py:55
  582.1 6.4 convolution_convert_fusion.1
  592.0 3.0 fusion.7
  595.8 3.0 copy-done.1
  600.1 5.3 multiply_reduce_fusion
  605.4 4.6 fusion.73
  610.0 6.6 copy.235
  616.6 3.7 copy.281
  622.4 2.6 fusion.48
  635.7 2.4 fusion.37
  638.1 6.3 copy.232
  648.8 3.2 copy-done.48
  653.1 16.0 %convolution_convert_fusion = bf16[2048,3072]{1,0:T(8,128)(2,1)} fusion(bf16[1024,2048]{1,0:T(8,128)(2,1)S(1)} %bitcast.266, bf16[1024,3072]{1,0:T(8,128)(2,1)S(1)} %constant_dynamic-update-slice_fusion), kind=kOutput, calls=%fused_computation | convolution fusion | flops 12891193344 | bytes 23068672 | tf_op jit(solution)/shard_map/dot_general | solution.py:46
  669.2 6.2 copy.241
  678.2 6.2 convolution_convert_fusion.3
  684.4 18.0 %fusion.90 = f32[1024,2048]{1,0:T(8,128)S(1)} fusion(bf16[1024,3072]{1,0:T(8,128)(2,1)} %copy-done.48, bf16[2048,3072]{1,0:T(8,128)(2,1)} %all-gather.6.cloned.1.call-done), kind=kOutput, calls=%fused_computation.225 | convolution fusion | flops 12884901888 | bytes 27262976 | tf_op jit(solution)/shard_map/dot_general | solution.py:46
  703.4 3.8 collective-permute-done.15
  712.8 4.1 all-to-all-start.3
  721.2 21.4 %all-to-all-done.3 = bf16[4,64,1024]{2,1,0:T(8,128)(2,1)} async-done(((bf16[4,64,1024]{2,1,0:T(8,128)(2,1)}), bf16[4,64,1024]{2,1,0:T(8,128)(2,1)}, u32[]{:S(2)}, u32[]{:S(2)}) %all-to-all-start.3) | async-done | bytes 524320 | tf_op jit(solution)/shard_map/all_to_all | solution.py:84
  748.2 2.7 fusion.24
  752.4 133.5 %reduce-scatter.8.cloned.1.call-done = bf16[256,3072]{1,0:T(8,128)(2,1)} async-done(((bf16[2048,3072]{1,0:T(8,128)(2,1)}), bf16[256,3072]{1,0:T(8,128)(2,1)}) %reduce-scatter.8.cloned.1.call-update) | async-done | bytes 1572880 | tf_op jit(solution)/shard_map/reduce_scatter | solution.py:92
  885.9 4.4 all-to-all-start.2
  890.2 4.0 fusion.72
  894.2 82.5 %reduce-scatter.10.cloned.1.call-done = bf16[128,2048]{1,0:T(8,128)(2,1)} async-done(((bf16[1024,2048]{1,0:T(8,128)(2,1)}), bf16[128,2048]{1,0:T(8,128)(2,1)}) %reduce-scatter.10.cloned.1.call-update) | async-done | bytes 524304 | tf_op jit(solution)/shard_map/reduce_scatter | solution.py:92
  978.4 3.3 add_convert_fusion.3
  981.7 132.5 %reduce-scatter.16.cloned.1.call-done = f32[64,4]{1,0:T(8,128)} async-done(((f32[2048,4]{1,0:T(8,128)}), f32[64,4]{1,0:T(8,128)}) %reduce-scatter.16.cloned.1.call-update) | async-done | bytes 1040
  (321 shorter events, 121.6 us)
Async XLA Ops:
  7.2 232.3 %all-gather.6.cloned.1.call-start = ((), (), s32[]{:S(2)}) async-start(), calls=%async_computation.9 | async-start | bytes 14155776 | tf_op jit(solution)/shard_map/all_gather | solution.py:88
  11.9 24.5 %copy-start.70 = (bf16[128,2048]{1,0:T(8,128)(2,1)S(1)}, bf16[128,2048]{1,0:T(8,128)(2,1)}, u32[]{:S(2)}) copy-start(bf16[128,2048]{1,0:T(8,128)(2,1)} %param.17) | copy-start | bytes 1572868
  12.0 26.0 %copy-start.64 = (bf16[64]{0:T(256)(128)(2,1)S(1)}, bf16[64]{0:T(256)(128)(2,1)}, u32[]{:S(2)}) copy-start(bf16[64]{0:T(256)(128)(2,1)} %param.19) | copy-start | bytes 388
  12.0 26.0 %copy-start.65 = (bf16[64]{0:T(256)(128)(2,1)S(1)}, bf16[64]{0:T(256)(128)(2,1)}, u32[]{:S(2)}) copy-start(bf16[64]{0:T(256)(128)(2,1)} %param.18) | copy-start | bytes 388
  12.0 26.0 %copy-start.66 = (bf16[64]{0:T(256)(128)(2,1)S(1)}, bf16[64]{0:T(256)(128)(2,1)}, u32[]{:S(2)}) copy-start(bf16[64]{0:T(256)(128)(2,1)} %param.15) | copy-start | bytes 388
  12.0 26.0 %copy-start.67 = (bf16[64]{0:T(256)(128)(2,1)S(1)}, bf16[64]{0:T(256)(128)(2,1)}, u32[]{:S(2)}) copy-start(bf16[64]{0:T(256)(128)(2,1)} %param.14) | copy-start | bytes 388
  12.0 132.2 %copy-start.4 = (bf16[256,2048]{1,0:T(8,128)(2,1)S(1)}, bf16[256,2048]{1,0:T(8,128)(2,1)}, u32[]{:S(2)}) copy-start(bf16[256,2048]{1,0:T(8,128)(2,1)} %param.11) | copy-start | bytes 3145732
  36.4 277.4 %all-gather.8.cloned.1.call-start = ((), (), s32[]{:S(2)}) async-start(), calls=%async_computation.10 | async-start | bytes 4718592 | tf_op jit(solution)/shard_map/all_gather | solution.py:88
  36.5 0.7 collective-permute-start.2
  145.4 3.7 copy-start.55
  146.9 10.4 copy-start.71
  146.9 26.2 %collective-permute-start = (bf16[1,256,2048]{2,1,0:T(8,128)(2,1)}, bf16[1,256,2048]{2,1,0:T(8,128)(2,1)S(1)}, u32[]{:S(2)}, u32[]{:S(2)}) collective-permute-start(bf16[1,256,2048]{2,1,0:T(8,128)(2,1)} %get-tuple-element.56), channel_id=1, source_target_pairs={{0,2},{1,3},{2,0},{3,1},{4,6},{5,7},{6,4},{7,5},{8,10},{9,11},{10,... | collective-permute-start | bytes 3145736 | tf_op jit(solution)/shard_map/ppermute | solution.py:55
  153.1 29.6 %all-to-all-start.1 = ((bf16[4,64,1024]{2,1,0:T(8,128)(2,1)}), bf16[4,64,1024]{2,1,0:T(8,128)(2,1)}, u32[]{:S(2)}, u32[]{:S(2)}) async-start(bf16[4,64,1024]{2,1,0:T(8,128)(2,1)} %reshape.737), calls=%async_computation.1 | async-start | bytes 1048576 | tf_op jit(solution)/shard_map/all_to_all | solution.py:84
  157.2 256.1 %all-gather.10.cloned.1.call-start = ((), (), s32[]{:S(2)}) async-start(), calls=%async_computation.11 | async-start | bytes 4718592 | tf_op jit(solution)/shard_map/all_gather | solution.py:88
  176.4 6.9 collective-permute-start.1
  178.4 114.1 %copy-start.61 = (f32[2]{0:T(128)}, f32[2]{0:T(128)S(1)}, u32[]{:S(2)}) copy-start(f32[2]{0:T(128)S(1)} %get-tuple-element.78) | copy-start | bytes 28
  178.5 113.1 %copy-start.59 = (f32[256,2]{0,1:T(2,128)}, f32[256,2]{0,1:T(2,128)S(1)}, u32[]{:S(2)}) copy-start(f32[256,2]{0,1:T(2,128)S(1)} %get-tuple-element.79) | copy-start | bytes 6148
  178.5 118.1 %copy-start.51 = (f32[256,2]{0,1:T(2,128)}, f32[256,2]{0,1:T(2,128)S(1)}, u32[]{:S(2)}) copy-start(f32[256,2]{0,1:T(2,128)S(1)} %get-tuple-element.80) | copy-start | bytes 6148
  179.5 117.2 %copy-start.72 = (bf16[4]{0:T(256)(128)(2,1)}, bf16[4]{0:T(256)(128)(2,1)S(1)}, u32[]{:S(2)}) copy-start(bf16[4]{0:T(256)(128)(2,1)S(1)} %pad.52.clone) | copy-start | bytes 28
  182.7 278.6 %all-gather.12.cloned.1.call-start = ((), (), s32[]{:S(2)}) async-start(), calls=%async_computation.12 | async-start | bytes 4718592 | tf_op jit(solution)/shard_map/all_gather | solution.py:88
  266.1 29.5 %copy-start.10 = (bf16[4,256,2,512]{3,2,1,0:T(2,128)(2,1)}, bf16[4,256,2,512]{3,2,1,0:T(2,128)(2,1)S(1)}, u32[]{:S(2)}) copy-start(bf16[4,256,2,512]{3,2,1,0:T(2,128)(2,1)S(1)} %reshape.733) | copy-start | bytes 6291460
  291.4 5.3 copy-start.23
  291.4 5.3 copy-start.25
  291.6 3.6 copy-start.16
  298.1 3.7 copy-start
  303.1 17.1 %copy-start.18 = (bf16[4,256,2,512]{1,3,2,0:T(8,128)(2,1)}, bf16[4,256,2,512]{1,3,2,0:T(8,128)(2,1)S(1)}, u32[]{:S(2)}) copy-start(bf16[4,256,2,512]{1,3,2,0:T(8,128)(2,1)S(1)} %multiply_convert_fusion.1) | copy-start | bytes 6291460
  320.2 4.0 copy-start.22
  324.2 4.4 collective-permute-start.3
  333.5 26.2 %collective-permute-start.4 = (bf16[1,256,2048]{2,1,0:T(8,128)(2,1)S(1)}, bf16[1,256,2048]{2,1,0:T(8,128)(2,1)}, u32[]{:S(2)}, u32[]{:S(2)}) collective-permute-start(bf16[1,256,2048]{2,1,0:T(8,128)(2,1)S(1)} %dynamic-slice_convert_fusion.4), channel_id=1, source_target_pairs={{0,2},{1,3},{2,0},{3,1},{4,6},{5,7},{6,4},{7,5},{8,10},{9,11},{10,... | collective-permute-start | bytes 3145736 | tf_op jit(solution)/shard_map/ppermute | solution.py:55
  335.1 377.7 %reduce-scatter.12.cloned.1.call-start = ((), (), s32[]{:S(2)}) async-start(), calls=%async_computation.15 | async-start | bytes 4718592 | tf_op jit(solution)/shard_map/reduce_scatter | solution.py:92
  335.1 46.9 %collective-permute-start.9 = (bf16[1,256,2048]{2,1,0:T(8,128)(2,1)}, bf16[1,256,2048]{2,1,0:T(8,128)(2,1)S(1)}, u32[]{:S(2)}, u32[]{:S(2)}) collective-permute-start(bf16[1,256,2048]{2,1,0:T(8,128)(2,1)} %bitcast.42), channel_id=1, source_target_pairs={{0,2},{1,3},{2,0},{3,1},{4,6},{5,7},{6,4},{7,5},{8,10},{9,11},{10,... | collective-permute-start | bytes 3145736 | tf_op jit(solution)/shard_map/ppermute | solution.py:55
  362.9 40.9 %collective-permute-start.5 = (bf16[1,256,2048]{2,1,0:T(8,128)(2,1)S(1)}, bf16[1,256,2048]{2,1,0:T(8,128)(2,1)S(1)}, u32[]{:S(2)}, u32[]{:S(2)}) collective-permute-start(bf16[1,256,2048]{2,1,0:T(8,128)(2,1)S(1)} %fusion.126), channel_id=1, source_target_pairs={{0,2},{1,3},{2,0},{3,1},{4,6},{5,7},{6,4},{7,5},{8,10},{9,11},{10,... | collective-permute-start | bytes 3145736 | tf_op jit(solution)/shard_map/ppermute | solution.py:55
  384.0 22.1 %collective-permute-start.10 = (bf16[2,256,2048]{2,1,0:T(8,128)(2,1)S(1)}, bf16[2,256,2048]{2,1,0:T(8,128)(2,1)S(1)}, u32[]{:S(2)}, u32[]{:S(2)}) collective-permute-start(bf16[2,256,2048]{2,1,0:T(8,128)(2,1)S(1)} %maximum_select_fusion.8), channel_id=1, source_target_pairs={{0,1},{1,0},{2,3},{3,2},{4,5},{5,4},{6,7},{7,6},{8,9},{9,8},{10,11... | collective-permute-start | bytes 6291464 | tf_op jit(solution)/shard_map/ppermute | solution.py:55
  404.1 6.2 collective-permute-start.6
  461.3 16.9 %copy-start.34 = (f32[1024,1024]{1,0:T(8,128)S(1)}, f32[1024,1024]{1,0:T(8,128)}, u32[]{:S(2)}) copy-start(f32[1024,1024]{1,0:T(8,128)} %fusion.86) | copy-start | bytes 12582916
  478.2 3.7 copy-start.33
  488.1 230.9 %reduce-scatter.14.cloned.1.call-start = ((), (), s32[]{:S(2)}) async-start(), calls=%async_computation.16 | async-start | bytes 4718592 | tf_op jit(solution)/shard_map/reduce_scatter | solution.py:92
  488.2 7.8 copy-start.69
  495.9 6.2 collective-permute-start.11
  502.0 4.4 collective-permute-start.7
  503.0 48.3 %copy-start.9 = (f32[2,256,2048]{2,1,0:T(8,128)}, f32[2,256,2048]{2,1,0:T(8,128)S(1)}, u32[]{:S(2)}) copy-start(f32[2,256,2048]{2,1,0:T(8,128)S(1)} %bitcast_add_fusion.1) | copy-start | bytes 12582916
  503.1 26.0 %collective-permute-start.12 = (bf16[1,256,2048]{2,1,0:T(8,128)(2,1)S(1)}, bf16[1,256,2048]{2,1,0:T(8,128)(2,1)S(1)}, u32[]{:S(2)}, u32[]{:S(2)}) collective-permute-start(bf16[1,256,2048]{2,1,0:T(8,128)(2,1)S(1)} %dynamic-slice_convert_fusion.2), channel_id=1, source_target_pairs={{0,2},{1,3},{2,0},{3,1},{4,6},{5,7},{6,4},{7,5},{8,10},{9,11},{10,... | collective-permute-start | bytes 3145736 | tf_op jit(solution)/shard_map/ppermute | solution.py:55
  509.0 42.2 %collective-permute-start.8 = (bf16[1,256,2048]{2,1,0:T(8,128)(2,1)S(1)}, bf16[1,256,2048]{2,1,0:T(8,128)(2,1)S(1)}, u32[]{:S(2)}, u32[]{:S(2)}) collective-permute-start(bf16[1,256,2048]{2,1,0:T(8,128)(2,1)S(1)} %dynamic-slice_convert_fusion.3), channel_id=1, source_target_pairs={{0,2},{1,3},{2,0},{3,1},{4,6},{5,7},{6,4},{7,5},{8,10},{9,11},{10,... | collective-permute-start | bytes 3145736 | tf_op jit(solution)/shard_map/ppermute | solution.py:55
  529.1 22.1 %copy-start.14 = (bf16[1,256,2048]{2,1,0:T(8,128)(2,1)}, bf16[1,256,2048]{2,1,0:T(8,128)(2,1)S(1)}, u32[]{:S(2)}) copy-start(bf16[1,256,2048]{2,1,0:T(8,128)(2,1)S(1)} %collective-permute-done.12) | copy-start | bytes 3145732
  555.5 26.5 %copy-start.32 = (bf16[2,2,256,2048]{3,2,1,0:T(8,128)(2,1)S(1)}, bf16[2,2,256,2048]{3,2,1,0:T(8,128)(2,1)}, u32[]{:S(2)}) copy-start(bf16[2,2,256,2048]{3,2,1,0:T(8,128)(2,1)} %copy.213) | copy-start | bytes 12582916
  555.5 24.8 %collective-permute-start.13 = (bf16[1,256,2048]{2,1,0:T(8,128)(2,1)S(1)}, bf16[1,256,2048]{2,1,0:T(8,128)(2,1)S(1)}, u32[]{:S(2)}, u32[]{:S(2)}) collective-permute-start(bf16[1,256,2048]{2,1,0:T(8,128)(2,1)S(1)} %fusion.124), channel_id=1, source_target_pairs={{0,2},{1,3},{2,0},{3,1},{4,6},{5,7},{6,4},{7,5},{8,10},{9,11},{10,... | collective-permute-start | bytes 3145736 | tf_op jit(solution)/shard_map/ppermute | solution.py:55
  582.0 10.0 collective-permute-start.14
  588.5 297.4 %reduce-scatter.8.cloned.1.call-start = ((), (), s32[]{:S(2)}) async-start(), calls=%async_computation.13 | async-start | bytes 14155776 | tf_op jit(solution)/shard_map/reduce_scatter | solution.py:92
  592.0 3.8 copy-start.68
  595.0 3.8 copy-start.1
  595.0 5.1 copy-start.3
  595.6 9.8 copy-start.30
  616.5 3.7 copy-start.12
  648.7 4.5 copy-start.29
  648.8 3.2 copy-start.48
  669.1 307.6 %reduce-scatter.10.cloned.1.call-start = ((), (), s32[]{:S(2)}) async-start(), calls=%async_computation.14 | async-start | bytes 4718592 | tf_op jit(solution)/shard_map/reduce_scatter | solution.py:92
  702.7 4.4 collective-permute-start.15
  710.1 7.0 copy-start.15
  711.3 34.6 %collective-permute-start.16 = (bf16[1,256,2048]{2,1,0:T(8,128)(2,1)}, bf16[1,256,2048]{2,1,0:T(8,128)(2,1)}, u32[]{:S(2)}, u32[]{:S(2)}) collective-permute-start(bf16[1,256,2048]{2,1,0:T(8,128)(2,1)} %dynamic-slice_convert_fusion.1), channel_id=1, source_target_pairs={{0,2},{1,3},{2,0},{3,1},{4,6},{5,7},{6,4},{7,5},{8,10},{9,11},{10,... | collective-permute-start | bytes 3145736 | tf_op jit(solution)/shard_map/ppermute | solution.py:55
  712.8 29.9 %all-to-all-start.3 = ((bf16[4,64,1024]{2,1,0:T(8,128)(2,1)}), bf16[4,64,1024]{2,1,0:T(8,128)(2,1)}, u32[]{:S(2)}, u32[]{:S(2)}) async-start(bf16[4,64,1024]{2,1,0:T(8,128)(2,1)} %bitcast.289), calls=%async_computation.6 | async-start | bytes 1048576 | tf_op jit(solution)/shard_map/all_to_all | solution.py:84
  716.9 397.3 %reduce-scatter.16.cloned.1.call-start = ((), (), s32[]{:S(2)}) async-start(), calls=%async_computation.17 | async-start | bytes 1081344
  748.2 4.1 copy-start.58
  885.9 232.7 %all-to-all-start.2 = ((bf16[4,64,3072]{2,1,0:T(8,128)(2,1)}), bf16[4,64,3072]{2,1,0:T(8,128)(2,1)}, u32[]{:S(2)}, u32[]{:S(2)}) async-start(bf16[4,64,3072]{2,1,0:T(8,128)(2,1)} %bitcast.286), calls=%async_computation.3 | async-start | bytes 3145728 | tf_op jit(solution)/shard_map/all_to_all | solution.py:84
  976.7 140.8 %collective-permute-start.17 = (bf16[128,2048]{1,0:T(8,128)(2,1)}, bf16[128,2048]{1,0:T(8,128)(2,1)S(1)}, u32[]{:S(2)}, u32[]{:S(2)}) collective-permute-start(bf16[128,2048]{1,0:T(8,128)(2,1)} %reduce-scatter.10.cloned.1.call-done), channel_id=1, source_target_pairs={{0,0},{4,1},{8,2},{12,3},{16,4},{20,5},{24,6},{28,7},{1,8},{5,9},{... | collective-permute-start | bytes 1572872 | tf_op jit(solution)/shard_map/ppermute | solution.py:207
  (41 other events, 71.2 us)
Sparse Core Ops, SparseCore 0:
  36.5 202.9 all-gather.5
  242.2 71.5 all-gather.7
  315.9 71.6 all-gather.9
  389.6 71.6 all-gather.11
  488.3 86.3 reduce-scatter.11
  588.6 86.5 reduce-scatter.13
  678.8 206.9 reduce-scatter.7
  889.5 87.1 reduce-scatter.9
  979.6 134.5 reduce-scatter.15
where the time goes:
time: 1140 us; the launch traced here: 1130 us
  waiting for transfers between devices  620 us (54%)
  matrix products  131 us (11%)
  blocking collectives  130 us (11%)
  local copies, waits for them, and re-layouts  127 us (11%)
  other arithmetic  78 us (7%)
  starting transfers between devices  26.5 us (2%)
  between operations  16.3 us (1%)
    reduce_scatter x4, waiting for transfers between devices, scatter_dp(): lax.psum_scatter(x.astype(bf16), 'dp', scatter_dimension=0, tiled=True)  216 us
    ppermute x16, waiting for transfers between devices, swap_seq(): return lax.ppermute(x, 'seq', [(i, i ^ bit) for i in range(size)])  150 us
    unnamed x10, waiting for transfers between devices  133 us
    dot_general x12, matrix products, dot(): return lax.dot_general(a, b, (dims, ((), ())), preferred_element_type=f32)  120 us
    all_gather x1, blocking collectives, local(): lax.all_gather(jnp.stack([norm1_gain, norm1_shift, norm2_gain, norm2_shif...  106 us
    all_gather x4, waiting for transfers between devices, gather_dp(): return lax.all_gather(x, 'dp', axis=0, tiled=True)  99.8 us
    unnamed x166, local copies, waits for them, and re-layouts  45.7 us
    all_to_all x1, blocking collectives, exchange_seq(): return lax.all_to_all(x, 'seq', 0, 0)  24.4 us
  transfers between devices with their start and end apart: 30, of which 17 were waited for; matrix products, arithmetic and copies ran while one was open for 24% of the time, Pallas kernels for 0%

commit v1 on v0

--- a/solution.py
+++ b/solution.py
@@ -11,6 +11,24 @@
 BOTH = ("dp", "seq")
 f32 = jnp.float32
 bf16 = jnp.bfloat16
+
+
+def collect(value, axis, dim):
+    ways, here, turn = (lax.axis_size(axis), lax.axis_index(axis), value.shape[dim])
+    lengths = [n * ways if d == dim else n for d, n in enumerate(value.shape)]
+    full = lax.dynamic_update_slice_in_dim(
+        jnp.zeros(lengths, value.dtype), value, here * turn, axis=dim
+    )
+    going_up = going_down = value
+    for far in range(1, ways // 2 + 1):
+        going_up = lax.ppermute(going_up, axis, [(d, (d + 1) % ways) for d in range(ways)])
+        full = lax.dynamic_update_slice_in_dim(full, going_up, (here - far) % ways * turn, axis=dim)
+        if 2 * far < ways:
+            going_down = lax.ppermute(going_down, axis, [(d, (d - 1) % ways) for d in range(ways)])
+            full = lax.dynamic_update_slice_in_dim(
+                full, going_down, (here + far) % ways * turn, axis=dim
+            )
+    return full
 
 
 def layer_norm(rows, row_gain, row_shift):
@@ -85,7 +103,7 @@
 
 
 def gather_dp(x):
-    return lax.all_gather(x, "dp", axis=0, tiled=True)
+    return collect(x, "dp", 0)
 
 
 def scatter_dp(x):

time: 1140 us -> 1380 us (1.21)
  waiting for transfers between devices: 620 us -> 806 us
  starting transfers between devices: 26.5 us -> 75.7 us
  local copies, waits for them, and re-layouts: 127 us -> 171 us
  blocking collectives: 130 us -> 86.5 us
    ppermute x0 -> x28, waiting for transfers between devices: none -> 360 us  [the longest x12 236 us: collect(): lax.ppermute(going_down, axis, [(d, (d - 1) % ways) for d in range(ways)])]
    all_gather x4 -> x0, waiting for transfers between devices: 99.8 us -> none  [gather_dp(): return lax.all_gather(x, 'dp', axis=0, tiled=True)]
    ppermute x16, waiting for transfers between devices: 150 us -> 76.7 us  [swap_seq(): return lax.ppermute(x, 'seq', [(i, i ^ bit) for i in range(size)])]
    ppermute x0 -> x28, starting transfers between devices: none -> 48.5 us  [the longest x12 36.8 us: collect(): lax.ppermute(going_down, axis, [(d, (d - 1) % ways) for d in range(ways)])]
    all_gather x1, blocking collectives: 106 us -> 57.7 us  [local(): lax.all_gather(jnp.stack([norm1_gain, norm1_shift, norm2_gain, norm2_shif...]
    dynamic_update_slice x0 -> x31, local copies, waits for them, and re-layouts: none -> 33.1 us  [the longest x15 18.9 us: collect(): lax.dynamic_update_slice_in_dim(full, going_up, (here - far) % ways * tur...]
    unnamed x166 -> x188, local copies, waits for them, and re-layouts: 45.7 us -> 44.7 us
    unnamed x10 -> x6, waiting for transfers between devices: 133 us -> 132 us
  transfers between devices with their start and end apart: 30 -> 54, of which waited for: 17 -> 27; matrix products, arithmetic and copies ran while one was open for 24% -> 17% of each run, Pallas kernels for 0% -> 0%
where the time goes in v1:
time: 1380 us; the launch traced here: 1370 us
  waiting for transfers between devices  806 us (58%)
  local copies, waits for them, and re-layouts  171 us (12%)
  matrix products  133 us (10%)
  blocking collectives  86.5 us (6%)
  other arithmetic  78.7 us (6%)
  starting transfers between devices  75.7 us (5%)
  between operations  17 us (1%)
    ppermute x12, waiting for transfers between devices, collect(): lax.ppermute(going_down, axis, [(d, (d - 1) % ways) for d in range(ways)])  236 us
    reduce_scatter x4, waiting for transfers between devices, scatter_dp(): lax.psum_scatter(x.astype(bf16), 'dp', scatter_dimension=0, tiled=True)  214 us
    unnamed x6, waiting for transfers between devices  132 us
    ppermute x16, waiting for transfers between devices, collect(): lax.ppermute(going_up, axis, [(d, (d + 1) % ways) for d in range(ways)])  124 us
    dot_general x12, matrix products, dot(): return lax.dot_general(a, b, (dims, ((), ())), preferred_element_type=f32)  122 us
    ppermute x16, waiting for transfers between devices, swap_seq(): return lax.ppermute(x, 'seq', [(i, i ^ bit) for i in range(size)])  76.7 us
    all_gather x1, blocking collectives, local(): lax.all_gather(jnp.stack([norm1_gain, norm1_shift, norm2_gain, norm2_shif...  57.7 us
    unnamed x188, local copies, waits for them, and re-layouts  44.7 us
  transfers between devices with their start and end apart: 54, of which 27 were waited for; matrix products, arithmetic and copies ran while one was open for 17% of the time, Pallas kernels for 0%

profile of v1, /device:TPU:0, one launch (start us, length us, event | category | flops | bytes accessed | tf_op | source)
XLA Modules:
  0.0 1368.1 jit_solution(7161195568212895980)
XLA Ops:
  7.2 6.0 collective-permute-start.29
  13.2 5.4 collective-permute-start.9
  28.9 57.7 %all-gather = bf16[32,64,4]{1,2,0:T(4,128)(2,1)S(1)} all-gather(bf16[1,64,4]{1,2,0:T(4,128)(2,1)S(1)} %maximum_bitcast_fusion.1), channel_id=1, replica_groups=mesh['dp'=8,'seq'=4] {'dp','seq'}, dimensions={0}, use_global_device_ids=true | all-gather | bytes 16896 | tf_op jit(solution)/shard_map/all_gather | solution.py:134
  98.5 4.5 collective-permute-start.11
  107.4 4.7 collective-permute-start.31
  117.8 4.0 maximum_select_fusion.4
  121.7 47.9 %collective-permute-done.11 = bf16[128,2048]{1,0:T(8,128)(2,1)S(1)} collective-permute-done((bf16[128,2048]{1,0:T(8,128)(2,1)}, bf16[128,2048]{1,0:T(8,128)(2,1)S(1)}, u32[]{:S(2)}, u32[]{:S(2)}) %collective-permute-start.11) | collective-permute-done | bytes 524320 | tf_op jit(solution)/shard_map/ppermute | solution.py:27
  174.8 39.8 %collective-permute-done.31 = bf16[128,2048]{1,0:T(8,128)(2,1)S(1)} collective-permute-done((bf16[128,2048]{1,0:T(8,128)(2,1)}, bf16[128,2048]{1,0:T(8,128)(2,1)S(1)}, u32[]{:S(2)}, u32[]{:S(2)}) %collective-permute-start.31) | collective-permute-done | bytes 524320 | tf_op jit(solution)/shard_map/ppermute | solution.py:27
  214.6 7.7 collective-permute-done.30
  222.3 3.9 collective-permute-start.33
  228.9 8.1 collective-permute-done.13
  237.1 6.2 broadcast_in_dim.45
  244.5 34.0 %collective-permute-done.12 = bf16[128,2048]{1,0:T(8,128)(2,1)} collective-permute-done((bf16[128,2048]{1,0:T(8,128)(2,1)}, bf16[128,2048]{1,0:T(8,128)(2,1)}, u32[]{:S(2)}, u32[]{:S(2)}) %collective-permute-start.12) | collective-permute-done | bytes 524320 | tf_op jit(solution)/shard_map/ppermute | solution.py:24
  278.5 3.9 collective-permute-start.15
  282.4 10.8 collective-permute-done.33
  295.3 5.6 collective-permute-done.32
  301.8 3.9 collective-permute-start.5
  307.6 8.1 collective-permute-done.15
  315.7 30.1 %collective-permute-done.14 = bf16[128,2048]{1,0:T(8,128)(2,1)S(1)} collective-permute-done((bf16[128,2048]{1,0:T(8,128)(2,1)}, bf16[128,2048]{1,0:T(8,128)(2,1)S(1)}, u32[]{:S(2)}, u32[]{:S(2)}) %collective-permute-start.14) | collective-permute-done | bytes 524320 | tf_op jit(solution)/shard_map/ppermute | solution.py:24
  351.8 5.3 collective-permute-done.34
  357.1 11.1 collective-permute-done.16
  372.0 33.1 %collective-permute-done.5 = bf16[256,3072]{1,0:T(8,128)(2,1)S(1)} collective-permute-done((bf16[256,3072]{1,0:T(8,128)(2,1)}, bf16[256,3072]{1,0:T(8,128)(2,1)S(1)}, u32[]{:S(2)}, u32[]{:S(2)}) %collective-permute-start.5) | collective-permute-done | bytes 1572896 | tf_op jit(solution)/shard_map/ppermute | solution.py:27
  417.6 56.9 %collective-permute-done.7 = bf16[256,3072]{1,0:T(8,128)(2,1)S(1)} collective-permute-done((bf16[256,3072]{1,0:T(8,128)(2,1)S(1)}, bf16[256,3072]{1,0:T(8,128)(2,1)S(1)}, u32[]{:S(2)}, u32[]{:S(2)}) %collective-permute-start.7) | collective-permute-done | bytes 1572896 | tf_op jit(solution)/shard_map/ppermute | solution.py:27
  476.3 15.6 %fusion.85 = f32[1024,3072]{1,0:T(8,128)} fusion(bf16[1024,2048]{1,0:T(8,128)(2,1)S(1)} %bitcast.268, bf16[2048,3072]{1,0:T(8,128)(2,1)S(1)} %constant_dynamic-update-slice_fusion.24), kind=kOutput, calls=%fused_computation.252 | convolution fusion | flops 12884901888 | bytes 29360128 | tf_op jit(solution)/shard_map/dot_general | solution.py:64
  491.9 3.8 slice.229
  495.7 4.8 slice.144
  500.6 4.7 fusion.77
  508.6 4.3 reshape.734
  512.8 6.6 reshape.732
  519.4 7.3 copy.200
  526.7 3.9 reshape.735
  545.6 7.2 fusion.8
  556.1 4.3 collective-permute-done.17
  568.1 28.7 %all_to_all.20 = bf16[4,64,1024]{2,1,0:T(8,128)(2,1)S(1)} all-to-all(bf16[4,64,1024]{2,1,0:T(8,128)(2,1)S(1)} %reshape.737), channel_id=1, replica_groups=mesh['dp'=8,'seq'=4] {'seq'}, dimensions={0} | all-to-all | bytes 1048576 | tf_op jit(solution)/shard_map/all_to_all | solution.py:102
  598.7 4.3 collective-permute-start.22
  603.0 16.4 %collective-permute-done.21 = bf16[256,1024]{1,0:T(8,128)(2,1)S(1)} collective-permute-done((bf16[256,1024]{1,0:T(8,128)(2,1)S(1)}, bf16[256,1024]{1,0:T(8,128)(2,1)S(1)}, u32[]{:S(2)}, u32[]{:S(2)}) %collective-permute-start.21) | collective-permute-done | bytes 524320 | tf_op jit(solution)/shard_map/ppermute | solution.py:24
  631.1 13.6 collective-permute-done.23
  647.9 10.5 collective-permute-done.24
  662.8 20.6 %collective-permute-done.26 = bf16[256,1024]{1,0:T(8,128)(2,1)S(1)} collective-permute-done((bf16[256,1024]{1,0:T(8,128)(2,1)S(1)}, bf16[256,1024]{1,0:T(8,128)(2,1)S(1)}, u32[]{:S(2)}, u32[]{:S(2)}) %collective-permute-start.26) | collective-permute-done | bytes 524320 | tf_op jit(solution)/shard_map/ppermute | solution.py:27
  687.0 4.5 fusion.86
  691.5 16.8 %add_convert_fusion.2 = (bf16[1024,1024]{1,0:T(8,128)(2,1)S(1)}, f32[1024,1024]{1,0:T(8,128)}) fusion(f32[1024,1024]{1,0:T(8,128)S(1)} %fusion.86, bf16[1024,2048]{1,0:T(8,128)(2,1)S(1)} %bitcast.272, bf16[1024,2048]{1,0:T(8,128)(2,1)} %get-tuple-element.89), kind=kOutput, calls=%fused_computation.31 | convolution fusion | flops 4370464768 | bytes 18874368 | tf_op jit(solution)/shard_map/dot_general | solution.py:64
  709.7 6.6 convolution_convert_fusion.2
  716.3 10.8 fusion.88
  732.4 6.8 fusion.87
  745.7 22.8 %collective-permute-done.40 = bf16[1,256,2048]{2,1,0:T(8,128)(2,1)S(1)} collective-permute-done((bf16[1,256,2048]{2,1,0:T(8,128)(2,1)S(1)}, bf16[1,256,2048]{2,1,0:T(8,128)(2,1)S(1)}, u32[]{:S(2)}, u32[]{:S(2)}) %collective-permute-start.40) | collective-permute-done | bytes 1048608 | tf_op jit(solution)/shard_map/ppermute | solution.py:73
  769.3 21.1 %collective-permute-done.36 = bf16[1,256,2048]{2,1,0:T(8,128)(2,1)S(1)} collective-permute-done((bf16[1,256,2048]{2,1,0:T(8,128)(2,1)S(1)}, bf16[1,256,2048]{2,1,0:T(8,128)(2,1)S(1)}, u32[]{:S(2)}, u32[]{:S(2)}) %collective-permute-start.36) | collective-permute-done | bytes 1048608 | tf_op jit(solution)/shard_map/ppermute | solution.py:73
  795.4 24.0 %collective-permute-done.41 = bf16[1,256,2048]{2,1,0:T(8,128)(2,1)S(1)} collective-permute-done((bf16[1,256,2048]{2,1,0:T(8,128)(2,1)S(1)}, bf16[1,256,2048]{2,1,0:T(8,128)(2,1)S(1)}, u32[]{:S(2)}, u32[]{:S(2)}) %collective-permute-start.41) | collective-permute-done | bytes 1048608 | tf_op jit(solution)/shard_map/ppermute | solution.py:73
  821.2 6.3 convolution_convert_fusion.1
  839.2 7.3 multiply_reduce_fusion
  846.5 4.6 fusion.73
  851.1 6.1 copy.235
  877.9 6.3 copy.232
  890.9 15.9 %convolution_convert_fusion = bf16[2048,3072]{1,0:T(8,128)(2,1)} fusion(bf16[1024,2048]{1,0:T(8,128)(2,1)S(1)} %bitcast.269, bf16[1024,3072]{1,0:T(8,128)(2,1)S(1)} %constant_dynamic-update-slice_fusion.32), kind=kOutput, calls=%fused_computation | convolution fusion | flops 12891193344 | bytes 23068672 | tf_op jit(solution)/shard_map/dot_general | solution.py:64
  906.9 6.2 copy.241
  915.9 6.3 convolution_convert_fusion.3
  922.3 17.9 %fusion.90 = f32[1024,2048]{1,0:T(8,128)S(1)} fusion(bf16[1024,3072]{1,0:T(8,128)(2,1)} %copy-done.58, bf16[2048,3072]{1,0:T(8,128)(2,1)} %copy-done.15), kind=kOutput, calls=%fused_computation.257 | convolution fusion | flops 12884901888 | bytes 27262976 | tf_op jit(solution)/shard_map/dot_general | solution.py:64
  941.1 3.8 collective-permute-done.43
  948.9 4.1 all-to-all-start.3
  957.4 22.8 %all-to-all-done.3 = bf16[4,64,1024]{2,1,0:T(8,128)(2,1)} async-done(((bf16[4,64,1024]{2,1,0:T(8,128)(2,1)}), bf16[4,64,1024]{2,1,0:T(8,128)(2,1)}, u32[]{:S(2)}, u32[]{:S(2)}) %all-to-all-start.3) | async-done | bytes 524320 | tf_op jit(solution)/shard_map/all_to_all | solution.py:102
  992.2 132.1 %reduce-scatter.8.cloned.1.call-done = bf16[256,3072]{1,0:T(8,128)(2,1)} async-done(((bf16[2048,3072]{1,0:T(8,128)(2,1)}), bf16[256,3072]{1,0:T(8,128)(2,1)}) %reduce-scatter.8.cloned.1.call-update) | async-done | bytes 1572880 | tf_op jit(solution)/shard_map/reduce_scatter | solution.py:110
  1124.3 4.3 all-to-all-start.2
  1128.6 4.0 fusion.72
  1132.6 82.4 %reduce-scatter.10.cloned.1.call-done = bf16[128,2048]{1,0:T(8,128)(2,1)} async-done(((bf16[1024,2048]{1,0:T(8,128)(2,1)}), bf16[128,2048]{1,0:T(8,128)(2,1)}) %reduce-scatter.10.cloned.1.call-update) | async-done | bytes 524304 | tf_op jit(solution)/shard_map/reduce_scatter | solution.py:110
  1219.9 132.4 %reduce-scatter.16.cloned.1.call-done = f32[64,4]{1,0:T(8,128)} async-done(((f32[2048,4]{1,0:T(8,128)}), f32[64,4]{1,0:T(8,128)}) %reduce-scatter.16.cloned.1.call-update) | async-done | bytes 1040
  (423 shorter events, 219.6 us)
Async XLA Ops:
  7.2 100.2 %collective-permute-start.29 = (bf16[128,2048]{1,0:T(8,128)(2,1)}, bf16[128,2048]{1,0:T(8,128)(2,1)}, u32[]{:S(2)}, u32[]{:S(2)}) collective-permute-start(bf16[128,2048]{1,0:T(8,128)(2,1)} %param.21), channel_id=1, source_target_pairs={{0,28},{4,0},{8,4},{12,8},{16,12},{20,16},{24,20},{28,24},{1,29},{... | collective-permute-start | bytes 1572872 | tf_op jit(solution)/shard_map/ppermute | solution.py:27
  13.2 94.2 %collective-permute-start.28 = (bf16[128,2048]{1,0:T(8,128)(2,1)}, bf16[128,2048]{1,0:T(8,128)(2,1)}, u32[]{:S(2)}, u32[]{:S(2)}) collective-permute-start(bf16[128,2048]{1,0:T(8,128)(2,1)} %param.21), channel_id=1, source_target_pairs={{0,4},{4,8},{8,12},{12,16},{16,20},{20,24},{24,28},{28,0},{1,5},{5... | collective-permute-start | bytes 1572872 | tf_op jit(solution)/shard_map/ppermute | solution.py:24
  13.2 85.3 %collective-permute-start.9 = (bf16[128,2048]{1,0:T(8,128)(2,1)}, bf16[128,2048]{1,0:T(8,128)(2,1)}, u32[]{:S(2)}, u32[]{:S(2)}) collective-permute-start(bf16[128,2048]{1,0:T(8,128)(2,1)} %param.17), channel_id=1, source_target_pairs={{0,0},{1,4},{2,8},{3,12},{4,16},{5,20},{6,24},{7,28},{8,1},{9,5},{... | collective-permute-start | bytes 1572872 | tf_op jit(solution)/shard_map/ppermute | solution.py:148
  24.5 73.6 %all-to-all-start = ((bf16[4,64,3072]{2,1,0:T(8,128)(2,1)}), bf16[4,64,3072]{2,1,0:T(8,128)(2,1)S(1)}, u32[]{:S(2)}, u32[]{:S(2)}) async-start(bf16[4,64,3072]{2,1,0:T(8,128)(2,1)} %copy.198), calls=%async_computation | async-start | bytes 3145728 | tf_op jit(solution)/shard_map/all_to_all | solution.py:102
  28.1 920.8 %reduce-scatter.12.cloned.1.call-start = ((), (), s32[]{:S(2)}) async-start(), calls=%async_computation.11 | async-start | bytes 4718592 | tf_op jit(solution)/shard_map/reduce_scatter | solution.py:110
  28.3 60.3 %copy-start.65 = (f32[256]{0:T(256)}, f32[256]{0:T(256)S(1)}, u32[]{:S(2)}) copy-start(f32[256]{0:T(256)S(1)} %broadcast_multiply_fusion.2) | copy-start | bytes 3076
  28.8 58.0 %copy-start.69 = (f32[256]{0:T(256)}, f32[256]{0:T(256)S(1)}, u32[]{:S(2)}) copy-start(f32[256]{0:T(256)S(1)} %fusion.25) | copy-start | bytes 3076
  28.8 63.2 %copy-start.56 = (bf16[128,2048]{1,0:T(8,128)(2,1)S(1)}, bf16[128,2048]{1,0:T(8,128)(2,1)}, u32[]{:S(2)}) copy-start(bf16[128,2048]{1,0:T(8,128)(2,1)} %param.21) | copy-start | bytes 1572868
  28.8 59.8 %copy-start.67 = (f32[256]{0:T(256)}, f32[256]{0:T(256)S(1)}, u32[]{:S(2)}) copy-start(f32[256]{0:T(256)S(1)} %fusion.62) | copy-start | bytes 3076
  88.6 27.3 %collective-permute-start = (bf16[1,256,2048]{2,1,0:T(8,128)(2,1)}, bf16[1,256,2048]{2,1,0:T(8,128)(2,1)}, u32[]{:S(2)}, u32[]{:S(2)}) collective-permute-start(bf16[1,256,2048]{2,1,0:T(8,128)(2,1)} %get-tuple-element.56), channel_id=1, source_target_pairs={{0,2},{1,3},{2,0},{3,1},{4,6},{5,7},{6,4},{7,5},{8,10},{9,11},{10,... | collective-permute-start | bytes 3145736 | tf_op jit(solution)/shard_map/ppermute | solution.py:73
  89.5 446.2 %copy-start.71 = (f32[256,2]{0,1:T(2,128)}, f32[256,2]{0,1:T(2,128)S(1)}, u32[]{:S(2)}) copy-start(f32[256,2]{0,1:T(2,128)S(1)} %get-tuple-element.79) | copy-start | bytes 6148
  89.5 449.7 %copy-start.63 = (f32[256,2]{0,1:T(2,128)}, f32[256,2]{0,1:T(2,128)S(1)}, u32[]{:S(2)}) copy-start(f32[256,2]{0,1:T(2,128)S(1)} %get-tuple-element.80) | copy-start | bytes 6148
  98.1 75.8 %collective-permute-start.2 = (bf16[256,3072]{1,0:T(8,128)(2,1)S(1)}, bf16[256,3072]{1,0:T(8,128)(2,1)}, u32[]{:S(2)}, u32[]{:S(2)}) collective-permute-start(bf16[256,3072]{1,0:T(8,128)(2,1)S(1)} %bitcast.254), channel_id=1, source_target_pairs={{0,4},{4,8},{8,12},{12,16},{16,20},{20,24},{24,28},{28,0},{1,5},{5... | collective-permute-start | bytes 4718600 | tf_op jit(solution)/shard_map/ppermute | solution.py:24
  98.2 438.4 %copy-start.73 = (f32[2]{0:T(128)}, f32[2]{0:T(128)S(1)}, u32[]{:S(2)}) copy-start(f32[2]{0:T(128)S(1)} %get-tuple-element.78) | copy-start | bytes 28
  98.5 440.7 %copy-start.81 = (bf16[4]{0:T(256)(128)(2,1)}, bf16[4]{0:T(256)(128)(2,1)S(1)}, u32[]{:S(2)}) copy-start(bf16[4]{0:T(256)(128)(2,1)S(1)} %pad.52.clone) | copy-start | bytes 28
  98.5 71.2 %collective-permute-start.11 = (bf16[128,2048]{1,0:T(8,128)(2,1)}, bf16[128,2048]{1,0:T(8,128)(2,1)S(1)}, u32[]{:S(2)}, u32[]{:S(2)}) collective-permute-start(bf16[128,2048]{1,0:T(8,128)(2,1)} %collective-permute-done.9), channel_id=1, source_target_pairs={{0,28},{4,0},{8,4},{12,8},{16,12},{20,16},{24,20},{28,24},{1,29},{... | collective-permute-start | bytes 1572872 | tf_op jit(solution)/shard_map/ppermute | solution.py:27
  107.4 62.3 %collective-permute-start.10 = (bf16[128,2048]{1,0:T(8,128)(2,1)}, bf16[128,2048]{1,0:T(8,128)(2,1)}, u32[]{:S(2)}, u32[]{:S(2)}) collective-permute-start(bf16[128,2048]{1,0:T(8,128)(2,1)} %collective-permute-done.9), channel_id=1, source_target_pairs={{0,4},{4,8},{8,12},{12,16},{16,20},{20,24},{24,28},{28,0},{1,5},{5... | collective-permute-start | bytes 1572872 | tf_op jit(solution)/shard_map/ppermute | solution.py:24
  107.4 107.2 %collective-permute-start.31 = (bf16[128,2048]{1,0:T(8,128)(2,1)}, bf16[128,2048]{1,0:T(8,128)(2,1)S(1)}, u32[]{:S(2)}, u32[]{:S(2)}) collective-permute-start(bf16[128,2048]{1,0:T(8,128)(2,1)} %collective-permute-done.29), channel_id=1, source_target_pairs={{0,28},{4,0},{8,4},{12,8},{16,12},{20,16},{24,20},{28,24},{1,29},{... | collective-permute-start | bytes 1572872 | tf_op jit(solution)/shard_map/ppermute | solution.py:27
  115.8 106.4 %collective-permute-start.30 = (bf16[128,2048]{1,0:T(8,128)(2,1)}, bf16[128,2048]{1,0:T(8,128)(2,1)}, u32[]{:S(2)}, u32[]{:S(2)}) collective-permute-start(bf16[128,2048]{1,0:T(8,128)(2,1)} %collective-permute-done.28), channel_id=1, source_target_pairs={{0,4},{4,8},{8,12},{12,16},{16,20},{20,24},{24,28},{28,0},{1,5},{5... | collective-permute-start | bytes 1572872 | tf_op jit(solution)/shard_map/ppermute | solution.py:24
  169.7 67.4 %collective-permute-start.13 = (bf16[128,2048]{1,0:T(8,128)(2,1)S(1)}, bf16[128,2048]{1,0:T(8,128)(2,1)S(1)}, u32[]{:S(2)}, u32[]{:S(2)}) collective-permute-start(bf16[128,2048]{1,0:T(8,128)(2,1)S(1)} %collective-permute-done.11), channel_id=1, source_target_pairs={{0,28},{4,0},{8,4},{12,8},{16,12},{20,16},{24,20},{28,24},{1,29},{... | collective-permute-start | bytes 1572872 | tf_op jit(solution)/shard_map/ppermute | solution.py:27
  169.7 132.2 %collective-permute-start.3 = (bf16[256,3072]{1,0:T(8,128)(2,1)S(1)}, bf16[256,3072]{1,0:T(8,128)(2,1)}, u32[]{:S(2)}, u32[]{:S(2)}) collective-permute-start(bf16[256,3072]{1,0:T(8,128)(2,1)S(1)} %bitcast.255), channel_id=1, source_target_pairs={{0,28},{4,0},{8,4},{12,8},{16,12},{20,16},{24,20},{28,24},{1,29},{... | collective-permute-start | bytes 4718600 | tf_op jit(solution)/shard_map/ppermute | solution.py:27
  174.0 174.3 %collective-permute-start.4 = (bf16[256,3072]{1,0:T(8,128)(2,1)}, bf16[256,3072]{1,0:T(8,128)(2,1)}, u32[]{:S(2)}, u32[]{:S(2)}) collective-permute-start(bf16[256,3072]{1,0:T(8,128)(2,1)} %collective-permute-done.2), channel_id=1, source_target_pairs={{0,4},{4,8},{8,12},{12,16},{16,20},{20,24},{24,28},{28,0},{1,5},{5... | collective-permute-start | bytes 4718600 | tf_op jit(solution)/shard_map/ppermute | solution.py:24
  214.6 63.9 %collective-permute-start.12 = (bf16[128,2048]{1,0:T(8,128)(2,1)}, bf16[128,2048]{1,0:T(8,128)(2,1)}, u32[]{:S(2)}, u32[]{:S(2)}) collective-permute-start(bf16[128,2048]{1,0:T(8,128)(2,1)} %collective-permute-done.10), channel_id=1, source_target_pairs={{0,4},{4,8},{8,12},{12,16},{16,20},{20,24},{24,28},{28,0},{1,5},{5... | collective-permute-start | bytes 1572872 | tf_op jit(solution)/shard_map/ppermute | solution.py:24
  222.3 71.0 %collective-permute-start.33 = (bf16[128,2048]{1,0:T(8,128)(2,1)S(1)}, bf16[128,2048]{1,0:T(8,128)(2,1)S(1)}, u32[]{:S(2)}, u32[]{:S(2)}) collective-permute-start(bf16[128,2048]{1,0:T(8,128)(2,1)S(1)} %collective-permute-done.31), channel_id=1, source_target_pairs={{0,28},{4,0},{8,4},{12,8},{16,12},{20,16},{24,20},{28,24},{1,29},{... | collective-permute-start | bytes 1572872 | tf_op jit(solution)/shard_map/ppermute | solution.py:27
  237.1 63.9 %collective-permute-start.32 = (bf16[128,2048]{1,0:T(8,128)(2,1)}, bf16[128,2048]{1,0:T(8,128)(2,1)}, u32[]{:S(2)}, u32[]{:S(2)}) collective-permute-start(bf16[128,2048]{1,0:T(8,128)(2,1)} %collective-permute-done.30), channel_id=1, source_target_pairs={{0,4},{4,8},{8,12},{12,16},{16,20},{20,24},{24,28},{28,0},{1,5},{5... | collective-permute-start | bytes 1572872 | tf_op jit(solution)/shard_map/ppermute | solution.py:24
  243.2 57.7 %copy-start.46 = (bf16[2,256,2048]{2,1,0:T(8,128)(2,1)S(1)}, bf16[2,256,2048]{2,1,0:T(8,128)(2,1)}, u32[]{:S(2)}) copy-start(bf16[2,256,2048]{2,1,0:T(8,128)(2,1)} %maximum_select_fusion.4) | copy-start | bytes 6291460
  278.5 37.3 %collective-permute-start.15 = (bf16[128,2048]{1,0:T(8,128)(2,1)S(1)}, bf16[128,2048]{1,0:T(8,128)(2,1)S(1)}, u32[]{:S(2)}, u32[]{:S(2)}) collective-permute-start(bf16[128,2048]{1,0:T(8,128)(2,1)S(1)} %collective-permute-done.13), channel_id=1, source_target_pairs={{0,28},{4,0},{8,4},{12,8},{16,12},{20,16},{24,20},{28,24},{1,29},{... | collective-permute-start | bytes 1572872 | tf_op jit(solution)/shard_map/ppermute | solution.py:27
  293.3 52.6 %collective-permute-start.14 = (bf16[128,2048]{1,0:T(8,128)(2,1)}, bf16[128,2048]{1,0:T(8,128)(2,1)S(1)}, u32[]{:S(2)}, u32[]{:S(2)}) collective-permute-start(bf16[128,2048]{1,0:T(8,128)(2,1)} %collective-permute-done.12), channel_id=1, source_target_pairs={{0,4},{4,8},{8,12},{12,16},{16,20},{20,24},{24,28},{28,0},{1,5},{5... | collective-permute-start | bytes 1572872 | tf_op jit(solution)/shard_map/ppermute | solution.py:24
  300.9 109.0 %collective-permute-start.1 = (bf16[2,256,2048]{2,1,0:T(8,128)(2,1)S(1)}, bf16[2,256,2048]{2,1,0:T(8,128)(2,1)S(1)}, u32[]{:S(2)}, u32[]{:S(2)}) collective-permute-start(bf16[2,256,2048]{2,1,0:T(8,128)(2,1)S(1)} %copy-done.46), channel_id=1, source_target_pairs={{0,1},{1,0},{2,3},{3,2},{4,5},{5,4},{6,7},{7,6},{8,9},{9,8},{10,11... | collective-permute-start | bytes 6291464 | tf_op jit(solution)/shard_map/ppermute | solution.py:73
  301.8 103.2 %collective-permute-start.5 = (bf16[256,3072]{1,0:T(8,128)(2,1)}, bf16[256,3072]{1,0:T(8,128)(2,1)S(1)}, u32[]{:S(2)}, u32[]{:S(2)}) collective-permute-start(bf16[256,3072]{1,0:T(8,128)(2,1)} %collective-permute-done.3), channel_id=1, source_target_pairs={{0,28},{4,0},{8,4},{12,8},{16,12},{20,16},{24,20},{28,24},{1,29},{... | collective-permute-start | bytes 4718600 | tf_op jit(solution)/shard_map/ppermute | solution.py:27
  315.7 41.4 %collective-permute-start.34 = (bf16[128,2048]{1,0:T(8,128)(2,1)}, bf16[128,2048]{1,0:T(8,128)(2,1)S(1)}, u32[]{:S(2)}, u32[]{:S(2)}) collective-permute-start(bf16[128,2048]{1,0:T(8,128)(2,1)} %collective-permute-done.32), channel_id=1, source_target_pairs={{0,4},{4,8},{8,12},{12,16},{16,20},{20,24},{24,28},{28,0},{1,5},{5... | collective-permute-start | bytes 1572872 | tf_op jit(solution)/shard_map/ppermute | solution.py:24
  345.9 22.4 %collective-permute-start.16 = (bf16[128,2048]{1,0:T(8,128)(2,1)S(1)}, bf16[128,2048]{1,0:T(8,128)(2,1)S(1)}, u32[]{:S(2)}, u32[]{:S(2)}) collective-permute-start(bf16[128,2048]{1,0:T(8,128)(2,1)S(1)} %collective-permute-done.14), channel_id=1, source_target_pairs={{0,4},{4,8},{8,12},{12,16},{16,20},{20,24},{24,28},{28,0},{1,5},{5... | collective-permute-start | bytes 1572872 | tf_op jit(solution)/shard_map/ppermute | solution.py:24
  348.3 60.0 %collective-permute-start.6 = (bf16[256,3072]{1,0:T(8,128)(2,1)}, bf16[256,3072]{1,0:T(8,128)(2,1)S(1)}, u32[]{:S(2)}, u32[]{:S(2)}) collective-permute-start(bf16[256,3072]{1,0:T(8,128)(2,1)} %collective-permute-done.4), channel_id=1, source_target_pairs={{0,4},{4,8},{8,12},{12,16},{16,20},{20,24},{24,28},{28,0},{1,5},{5... | collective-permute-start | bytes 4718600 | tf_op jit(solution)/shard_map/ppermute | solution.py:24
  405.0 69.5 %collective-permute-start.7 = (bf16[256,3072]{1,0:T(8,128)(2,1)S(1)}, bf16[256,3072]{1,0:T(8,128)(2,1)S(1)}, u32[]{:S(2)}, u32[]{:S(2)}) collective-permute-start(bf16[256,3072]{1,0:T(8,128)(2,1)S(1)} %collective-permute-done.5), channel_id=1, source_target_pairs={{0,28},{4,0},{8,4},{12,8},{16,12},{20,16},{24,20},{28,24},{1,29},{... | collective-permute-start | bytes 4718600 | tf_op jit(solution)/shard_map/ppermute | solution.py:27
  408.2 66.5 %collective-permute-start.8 = (bf16[256,3072]{1,0:T(8,128)(2,1)S(1)}, bf16[256,3072]{1,0:T(8,128)(2,1)}, u32[]{:S(2)}, u32[]{:S(2)}) collective-permute-start(bf16[256,3072]{1,0:T(8,128)(2,1)S(1)} %collective-permute-done.6), channel_id=1, source_target_pairs={{0,4},{4,8},{8,12},{12,16},{16,20},{20,24},{24,28},{28,0},{1,5},{5... | collective-permute-start | bytes 4718600 | tf_op jit(solution)/shard_map/ppermute | solution.py:24
  414.5 61.8 %copy-start.31 = (bf16[2,2,256,2048]{3,2,1,0:T(8,128)(2,1)}, bf16[2,2,256,2048]{3,2,1,0:T(8,128)(2,1)S(1)}, u32[]{:S(2)}) copy-start(bf16[2,2,256,2048]{3,2,1,0:T(8,128)(2,1)S(1)} %copy.197) | copy-start | bytes 12582916
  556.1 4.3 collective-permute-start.17
  566.0 56.0 %collective-permute-start.18 = (bf16[1,256,2048]{2,1,0:T(8,128)(2,1)S(1)}, bf16[1,256,2048]{2,1,0:T(8,128)(2,1)}, u32[]{:S(2)}, u32[]{:S(2)}) collective-permute-start(bf16[1,256,2048]{2,1,0:T(8,128)(2,1)S(1)} %dynamic-slice_convert_fusion.4), channel_id=1, source_target_pairs={{0,2},{1,3},{2,0},{3,1},{4,6},{5,7},{6,4},{7,5},{8,10},{9,11},{10,... | collective-permute-start | bytes 3145736 | tf_op jit(solution)/shard_map/ppermute | solution.py:73
  596.9 22.5 %collective-permute-start.21 = (bf16[256,1024]{1,0:T(8,128)(2,1)S(1)}, bf16[256,1024]{1,0:T(8,128)(2,1)S(1)}, u32[]{:S(2)}, u32[]{:S(2)}) collective-permute-start(bf16[256,1024]{1,0:T(8,128)(2,1)S(1)} %bitcast.286), channel_id=1, source_target_pairs={{0,4},{4,8},{8,12},{12,16},{16,20},{20,24},{24,28},{28,0},{1,5},{5... | collective-permute-start | bytes 1572872 | tf_op jit(solution)/shard_map/ppermute | solution.py:24
  597.3 29.4 %collective-permute-start.37 = (bf16[1,256,2048]{2,1,0:T(8,128)(2,1)}, bf16[1,256,2048]{2,1,0:T(8,128)(2,1)S(1)}, u32[]{:S(2)}, u32[]{:S(2)}) collective-permute-start(bf16[1,256,2048]{2,1,0:T(8,128)(2,1)} %bitcast.42), channel_id=1, source_target_pairs={{0,2},{1,3},{2,0},{3,1},{4,6},{5,7},{6,4},{7,5},{8,10},{9,11},{10,... | collective-permute-start | bytes 3145736 | tf_op jit(solution)/shard_map/ppermute | solution.py:73
  598.7 29.9 %collective-permute-start.22 = (bf16[256,1024]{1,0:T(8,128)(2,1)S(1)}, bf16[256,1024]{1,0:T(8,128)(2,1)S(1)}, u32[]{:S(2)}, u32[]{:S(2)}) collective-permute-start(bf16[256,1024]{1,0:T(8,128)(2,1)S(1)} %bitcast.287), channel_id=1, source_target_pairs={{0,28},{4,0},{8,4},{12,8},{16,12},{20,16},{24,20},{28,24},{1,29},{... | collective-permute-start | bytes 1572872 | tf_op jit(solution)/shard_map/ppermute | solution.py:27
  619.4 25.3 %collective-permute-start.23 = (bf16[256,1024]{1,0:T(8,128)(2,1)S(1)}, bf16[256,1024]{1,0:T(8,128)(2,1)S(1)}, u32[]{:S(2)}, u32[]{:S(2)}) collective-permute-start(bf16[256,1024]{1,0:T(8,128)(2,1)S(1)} %collective-permute-done.21), channel_id=1, source_target_pairs={{0,4},{4,8},{8,12},{12,16},{16,20},{20,24},{24,28},{28,0},{1,5},{5... | collective-permute-start | bytes 1572872 | tf_op jit(solution)/shard_map/ppermute | solution.py:24
  625.2 35.2 %collective-permute-start.19 = (bf16[1,256,2048]{2,1,0:T(8,128)(2,1)S(1)}, bf16[1,256,2048]{2,1,0:T(8,128)(2,1)S(1)}, u32[]{:S(2)}, u32[]{:S(2)}) collective-permute-start(bf16[1,256,2048]{2,1,0:T(8,128)(2,1)S(1)} %fusion.126), channel_id=1, source_target_pairs={{0,2},{1,3},{2,0},{3,1},{4,6},{5,7},{6,4},{7,5},{8,10},{9,11},{10,... | collective-permute-start | bytes 3145736 | tf_op jit(solution)/shard_map/ppermute | solution.py:73
  628.5 55.1 %collective-permute-start.38 = (bf16[2,256,2048]{2,1,0:T(8,128)(2,1)S(1)}, bf16[2,256,2048]{2,1,0:T(8,128)(2,1)S(1)}, u32[]{:S(2)}, u32[]{:S(2)}) collective-permute-start(bf16[2,256,2048]{2,1,0:T(8,128)(2,1)S(1)} %maximum_select_fusion.8), channel_id=1, source_target_pairs={{0,1},{1,0},{2,3},{3,2},{4,5},{5,4},{6,7},{7,6},{8,9},{9,8},{10,11... | collective-permute-start | bytes 6291464 | tf_op jit(solution)/shard_map/ppermute | solution.py:73
  628.6 29.7 %collective-permute-start.24 = (bf16[256,1024]{1,0:T(8,128)(2,1)S(1)}, bf16[256,1024]{1,0:T(8,128)(2,1)S(1)}, u32[]{:S(2)}, u32[]{:S(2)}) collective-permute-start(bf16[256,1024]{1,0:T(8,128)(2,1)S(1)} %collective-permute-done.22), channel_id=1, source_target_pairs={{0,28},{4,0},{8,4},{12,8},{16,12},{20,16},{24,20},{28,24},{1,29},{... | collective-permute-start | bytes 1572872 | tf_op jit(solution)/shard_map/ppermute | solution.py:27
  644.7 13.7 collective-permute-start.25
  658.3 25.1 %collective-permute-start.26 = (bf16[256,1024]{1,0:T(8,128)(2,1)S(1)}, bf16[256,1024]{1,0:T(8,128)(2,1)S(1)}, u32[]{:S(2)}, u32[]{:S(2)}) collective-permute-start(bf16[256,1024]{1,0:T(8,128)(2,1)S(1)} %collective-permute-done.24), channel_id=1, source_target_pairs={{0,28},{4,0},{8,4},{12,8},{16,12},{20,16},{24,20},{28,24},{1,29},{... | collective-permute-start | bytes 1572872 | tf_op jit(solution)/shard_map/ppermute | solution.py:27
  658.4 25.2 %collective-permute-start.27 = (bf16[256,1024]{1,0:T(8,128)(2,1)S(1)}, bf16[256,1024]{1,0:T(8,128)(2,1)S(1)}, u32[]{:S(2)}, u32[]{:S(2)}) collective-permute-start(bf16[256,1024]{1,0:T(8,128)(2,1)S(1)} %collective-permute-done.25), channel_id=1, source_target_pairs={{0,4},{4,8},{8,12},{12,16},{16,20},{20,24},{24,28},{28,0},{1,5},{5... | collective-permute-start | bytes 1572872 | tf_op jit(solution)/shard_map/ppermute | solution.py:24
  660.7 25.0 %collective-permute-start.20 = (bf16[2,256,2048]{2,1,0:T(8,128)(2,1)S(1)}, bf16[2,256,2048]{2,1,0:T(8,128)(2,1)S(1)}, u32[]{:S(2)}, u32[]{:S(2)}) collective-permute-start(bf16[2,256,2048]{2,1,0:T(8,128)(2,1)S(1)} %maximum_select_fusion.6), channel_id=1, source_target_pairs={{0,1},{1,0},{2,3},{3,2},{4,5},{5,4},{6,7},{7,6},{8,9},{9,8},{10,11... | collective-permute-start | bytes 6291464 | tf_op jit(solution)/shard_map/ppermute | solution.py:73
  729.5 225.8 %reduce-scatter.14.cloned.1.call-start = ((), (), s32[]{:S(2)}) async-start(), calls=%async_computation.12 | async-start | bytes 4718592 | tf_op jit(solution)/shard_map/reduce_scatter | solution.py:110
  732.3 7.5 collective-permute-start.39
  739.6 4.2 collective-permute-start.35
  742.5 26.0 %collective-permute-start.40 = (bf16[1,256,2048]{2,1,0:T(8,128)(2,1)S(1)}, bf16[1,256,2048]{2,1,0:T(8,128)(2,1)S(1)}, u32[]{:S(2)}, u32[]{:S(2)}) collective-permute-start(bf16[1,256,2048]{2,1,0:T(8,128)(2,1)S(1)} %dynamic-slice_convert_fusion.2), channel_id=1, source_target_pairs={{0,2},{1,3},{2,0},{3,1},{4,6},{5,7},{6,4},{7,5},{8,10},{9,11},{10,... | collective-permute-start | bytes 3145736 | tf_op jit(solution)/shard_map/ppermute | solution.py:73
  744.8 45.6 %collective-permute-start.36 = (bf16[1,256,2048]{2,1,0:T(8,128)(2,1)S(1)}, bf16[1,256,2048]{2,1,0:T(8,128)(2,1)S(1)}, u32[]{:S(2)}, u32[]{:S(2)}) collective-permute-start(bf16[1,256,2048]{2,1,0:T(8,128)(2,1)S(1)} %dynamic-slice_convert_fusion.3), channel_id=1, source_target_pairs={{0,2},{1,3},{2,0},{3,1},{4,6},{5,7},{6,4},{7,5},{8,10},{9,11},{10,... | collective-permute-start | bytes 3145736 | tf_op jit(solution)/shard_map/ppermute | solution.py:73
  794.7 24.7 %collective-permute-start.41 = (bf16[1,256,2048]{2,1,0:T(8,128)(2,1)S(1)}, bf16[1,256,2048]{2,1,0:T(8,128)(2,1)S(1)}, u32[]{:S(2)}, u32[]{:S(2)}) collective-permute-start(bf16[1,256,2048]{2,1,0:T(8,128)(2,1)S(1)} %fusion.124), channel_id=1, source_target_pairs={{0,2},{1,3},{2,0},{3,1},{4,6},{5,7},{6,4},{7,5},{8,10},{9,11},{10,... | collective-permute-start | bytes 3145736 | tf_op jit(solution)/shard_map/ppermute | solution.py:73
  821.1 9.8 collective-permute-start.42
  827.4 296.8 %reduce-scatter.8.cloned.1.call-start = ((), (), s32[]{:S(2)}) async-start(), calls=%async_computation.9 | async-start | bytes 14155776 | tf_op jit(solution)/shard_map/reduce_scatter | solution.py:110
  906.9 308.1 %reduce-scatter.10.cloned.1.call-start = ((), (), s32[]{:S(2)}) async-start(), calls=%async_computation.10 | async-start | bytes 4718592 | tf_op jit(solution)/shard_map/reduce_scatter | solution.py:110
  940.5 4.3 collective-permute-start.43
  948.9 36.9 %collective-permute-start.44 = (bf16[1,256,2048]{2,1,0:T(8,128)(2,1)}, bf16[1,256,2048]{2,1,0:T(8,128)(2,1)}, u32[]{:S(2)}, u32[]{:S(2)}) collective-permute-start(bf16[1,256,2048]{2,1,0:T(8,128)(2,1)} %dynamic-slice_convert_fusion.1), channel_id=1, source_target_pairs={{0,2},{1,3},{2,0},{3,1},{4,6},{5,7},{6,4},{7,5},{8,10},{9,11},{10,... | collective-permute-start | bytes 3145736 | tf_op jit(solution)/shard_map/ppermute | solution.py:73
  948.9 31.4 %all-to-all-start.3 = ((bf16[4,64,1024]{2,1,0:T(8,128)(2,1)}), bf16[4,64,1024]{2,1,0:T(8,128)(2,1)}, u32[]{:S(2)}, u32[]{:S(2)}) async-start(bf16[4,64,1024]{2,1,0:T(8,128)(2,1)} %bitcast.296), calls=%async_computation.6 | async-start | bytes 1048576 | tf_op jit(solution)/shard_map/all_to_all | solution.py:102
  953.0 399.3 %reduce-scatter.16.cloned.1.call-start = ((), (), s32[]{:S(2)}) async-start(), calls=%async_computation.13 | async-start | bytes 1081344
  1124.3 232.4 %all-to-all-start.2 = ((bf16[4,64,3072]{2,1,0:T(8,128)(2,1)}), bf16[4,64,3072]{2,1,0:T(8,128)(2,1)}, u32[]{:S(2)}, u32[]{:S(2)}) async-start(bf16[4,64,3072]{2,1,0:T(8,128)(2,1)} %bitcast.293), calls=%async_computation.3 | async-start | bytes 3145728 | tf_op jit(solution)/shard_map/all_to_all | solution.py:102
  1215.0 140.7 %collective-permute-start.45 = (bf16[128,2048]{1,0:T(8,128)(2,1)}, bf16[128,2048]{1,0:T(8,128)(2,1)S(1)}, u32[]{:S(2)}, u32[]{:S(2)}) collective-permute-start(bf16[128,2048]{1,0:T(8,128)(2,1)} %reduce-scatter.10.cloned.1.call-done), channel_id=1, source_target_pairs={{0,0},{4,1},{8,2},{12,3},{16,4},{20,5},{24,6},{28,7},{1,8},{5,9},{... | collective-permute-start | bytes 1572872 | tf_op jit(solution)/shard_map/ppermute | solution.py:225
  (76 other events, 506.6 us)
Sparse Core Ops, SparseCore 0:
  729.7 85.7 reduce-scatter.11
  827.6 85.9 reduce-scatter.13
  917.2 207.0 reduce-scatter.7
  1127.8 87.1 reduce-scatter.9
  1217.7 134.5 reduce-scatter.15
